TPU v7x, 256 devices: a whole 4x4x8 slice. The times are simulated.
256 devices in a mesh: context: 32 (over z, x_lo, core), tensor: 8 (over x_hi, y).
Axes of the slice: x: 4 (x_hi: 2, x_lo: 2; x = x_hi * 2 + x_lo), y: 4, z: 8, core: 2. Of those that a mesh axis runs over, the one named last changes fastest.
Arguments:
- activations: bfloat16 [6144, 5120], P(('context', 'tensor')), may hold values from -6 to 6
- queries: bfloat16 [6144, 5120], P('context', 'tensor'), may hold values from -44 to 44
- key_weight: bfloat16 [5120, 1024], P(None, 'tensor'), may hold values from -0.5 to 1.1
- value_projection_weight: bfloat16 [5120, 1024], P(None, 'tensor'), may hold values from -0.078125 to 0.078125
- output_gradient: bfloat16 [6144, 5120], P('context', 'tensor'), may hold values from -6 to 6
- span_order: int32 [64], replicated, may hold values from 0 to 63, as said below
- doc_ids: int32 [6144], replicated, may hold values from 0 to 4, as said below
Outputs:
- attended: bfloat16 [6144, 5120], P('context', 'tensor')
- grad_queries: bfloat16 [6144, 5120], P('context', 'tensor')
- grad_inputs: bfloat16 [6144, 5120], P(('context', 'tensor'))
- grad_key_weight: float32 [5120, 1024], P('context', 'tensor')
- grad_value_weight: float32 [5120, 1024], P('context', 'tensor')
Inputs may be any that keep to these rules, and one draw needn't show every extreme that they name: `span_order`: each number once. `doc_ids`: taken in order of positions, the document numbers never fall; one document holds exactly 3072 positions and none holds more.
All inputs are finite; a program needn't handle non-finite values.
Results may differ from a plain program's by a relative error of at most 0.02.
Values may be sent and summed in bfloat16 or wider, within the bound.
No kernel may reach another device: no remote copies, remote signals or barrier semaphores. Data moves between devices by JAX's collectives and lax.ppermute only.
A program may use at most 192 MiB of HBM per device.

v0:
```python
import math
import jax
import jax.numpy as jnp
from jax import lax
from jax.sharding import PartitionSpec as P

HEAD_SIZE = 128
SPAN = 96


def on_device(
    activations, queries, key_weight, value_projection_weight, output_gradient, span_order, doc_ids
):
    local_rows = lax.all_gather(activations, "tensor", axis=0, tiled=True)
    shard_len = local_rows.shape[0]
    seq_len = doc_ids.shape[0]
    head_dim = HEAD_SIZE
    kv_width = key_weight.shape[1]
    kv_heads = kv_width // head_dim
    heads_per_group = queries.shape[1] // kv_width
    inv_root = 1.0 / math.sqrt(head_dim)
    key_local = jnp.dot(local_rows, key_weight, preferred_element_type=jnp.float32).astype(
        jnp.bfloat16
    )
    value_local = jnp.dot(
        local_rows, value_projection_weight, preferred_element_type=jnp.float32
    ).astype(jnp.bfloat16)
    row_ids = jnp.arange(seq_len, dtype=jnp.int32)
    span_match = (row_ids // SPAN)[:, None] == jnp.arange(span_order.shape[0], dtype=jnp.int32)[
        None, :
    ]
    all_pos = jnp.sum(jnp.where(span_match, span_order[None, :], 0), axis=1) * SPAN + row_ids % SPAN
    first_row = lax.axis_index("context") * shard_len
    query_pos = lax.dynamic_slice_in_dim(all_pos, first_row, shard_len)
    query_doc = lax.dynamic_slice_in_dim(doc_ids, first_row, shard_len)
    query_heads = queries.reshape(shard_len, kv_heads, heads_per_group, head_dim)
    grad_heads = output_gradient.reshape(shard_len, kv_heads, heads_per_group, head_dim)

    def visible():
        pair_mask = (query_doc[:, None] == doc_ids[None, :]) & (
            all_pos[None, :] <= query_pos[:, None]
        )
        return pair_mask[:, None, None, :]

    def scores_of(key_heads_split):
        return (
            jnp.einsum(
                "sgjd,ngd->sgjn", query_heads, key_heads_split, preferred_element_type=jnp.float32
            )
            * inv_root
        )

    stats_shape = (shard_len, kv_heads, heads_per_group)
    run_max = jnp.full(stats_shape, -1e30, jnp.float32)
    key_piece = lax.all_gather(key_local, "context", axis=0, tiled=True)
    value_piece = lax.all_gather(value_local, "context", axis=0, tiled=True)
    piece_len = key_piece.shape[0]
    pair_mask = visible()
    scores = scores_of(key_piece.reshape(piece_len, kv_heads, head_dim))
    new_max = jnp.maximum(run_max, jnp.max(jnp.where(pair_mask, scores, -1e30), axis=3))
    weights = jnp.where(pair_mask, jnp.exp(scores - new_max[..., None]), 0.0)
    value_heads_split = value_piece.reshape(piece_len, kv_heads, head_dim)
    summed = jnp.einsum(
        "sgjn,ngd->sgjd",
        weights.astype(jnp.bfloat16),
        value_heads_split,
        preferred_element_type=jnp.float32,
    )
    final_sum = jnp.sum(weights, axis=3)
    attended_low = (summed / final_sum[..., None]).astype(jnp.bfloat16)
    log_totals = new_max + jnp.log(final_sum)
    row_delta = jnp.sum(grad_heads.astype(jnp.float32) * attended_low.astype(jnp.float32), axis=3)
    key_piece = lax.all_gather(key_local, "context", axis=0, tiled=True)
    value_piece = lax.all_gather(value_local, "context", axis=0, tiled=True)
    piece_len = key_piece.shape[0]
    score_piece_len = key_piece.shape[0]
    pair_mask = visible()
    key_heads_split = key_piece.reshape(score_piece_len, kv_heads, head_dim)
    value_heads_split = value_piece.reshape(score_piece_len, kv_heads, head_dim)
    scores = scores_of(key_heads_split)
    probs = jnp.where(pair_mask, jnp.exp(scores - log_totals[..., None]), 0.0)
    grad_probs = jnp.einsum(
        "sgjd,ngd->sgjn", grad_heads, value_heads_split, preferred_element_type=jnp.float32
    )
    grad_scores = (probs * (grad_probs - row_delta[..., None]) * inv_root).astype(jnp.bfloat16)
    probs, grad_scores, key_heads_split = (probs, grad_scores, key_heads_split)
    grad_v_part = jnp.einsum(
        "sgjn,sgjd->ngd", probs.astype(jnp.bfloat16), grad_heads, preferred_element_type=jnp.float32
    )
    grad_q = jnp.einsum(
        "sgjn,ngd->sgjd", grad_scores, key_heads_split, preferred_element_type=jnp.float32
    )
    grad_k_part = jnp.einsum(
        "sgjn,sgjd->ngd", grad_scores, query_heads, preferred_element_type=jnp.float32
    )
    grad_k_buf = grad_k_part.reshape(piece_len, kv_width)
    grad_v_buf = grad_v_part.reshape(piece_len, kv_width)
    grad_q, grad_k_buf, grad_v_buf = (grad_q, grad_k_buf, grad_v_buf)
    grad_k_own, grad_v_own = (
        lax.psum_scatter(
            grad_k_buf.astype(jnp.bfloat16), "context", scatter_dimension=0, tiled=True
        ).astype(jnp.float32),
        lax.psum_scatter(
            grad_v_buf.astype(jnp.bfloat16), "context", scatter_dimension=0, tiled=True
        ).astype(jnp.float32),
    )
    grad_k_low = grad_k_own.astype(jnp.bfloat16)
    grad_v_low = grad_v_own.astype(jnp.bfloat16)
    grad_inputs = lax.psum_scatter(
        (
            jnp.dot(grad_k_low, key_weight.T, preferred_element_type=jnp.float32)
            + jnp.dot(grad_v_low, value_projection_weight.T, preferred_element_type=jnp.float32)
        ).astype(jnp.bfloat16),
        "tensor",
        scatter_dimension=0,
        tiled=True,
    )
    grad_kv = jnp.concatenate([grad_k_low, grad_v_low], axis=1)
    partial_grads = lax.dot_general(
        local_rows, grad_kv, (((0,), (0,)), ((), ())), preferred_element_type=jnp.float32
    )
    weight_grads = lax.psum_scatter(
        partial_grads.astype(jnp.bfloat16), "context", scatter_dimension=0, tiled=True
    ).astype(jnp.float32)
    attended = attended_low.reshape(shard_len, heads_per_group * kv_width)
    grad_queries = grad_q.astype(jnp.bfloat16).reshape(shard_len, heads_per_group * kv_width)
    return (
        attended,
        grad_queries,
        grad_inputs,
        weight_grads[:, :kv_width],
        weight_grads[:, kv_width:],
    )


def solution(mesh):
    return jax.shard_map(
        on_device,
        mesh=mesh,
        in_specs=(
            P(("context", "tensor"), None),
            P("context", "tensor"),
            P(None, "tensor"),
            P(None, "tensor"),
            P("context", "tensor"),
            P(),
            P(),
        ),
        out_specs=(
            P("context", "tensor"),
            P("context", "tensor"),
            P(("context", "tensor"), None),
            P("context", "tensor"),
            P("context", "tensor"),
        ),
        check_vma=False,
    )
```

profile of v0, /device:TPU:32, one launch (start us, length us, event | category | flops | bytes accessed | tf_op | source)
XLA Modules:
  0.0 701.8 jit_solution(13686100925459275635)
XLA Ops:
  7.2 0.0 all-gather.4.cloned.1.call-start
  7.3 0.7 all-gather.4.cloned.1.call-update
  7.9 0.0 all-gather.8.cloned.1.call-start
  8.0 62.8 %all-gather.4.cloned.1.call-done = bf16[192,5120]{1,0:T(8,128)(2,1)} async-done(((bf16[24,5120]{1,0:T(8,128)(2,1)}), bf16[192,5120]{1,0:T(8,128)(2,1)}) %all-gather.4.cloned.1.call-update) | async-done | bytes 1966096 | tf_op jit(solution)/shard_map/all_gather | solution.py:14
  70.8 3.0 convolution_convert_fusion.1
  73.8 0.0 all-gather.8.cloned.1.call-update
  73.8 0.0 all-gather.6.cloned.1.call-start
  73.9 2.0 copy.51
  75.8 0.9 copy.49
  76.7 2.1 copy.52
  78.9 0.3 select_reduce_fusion
  79.2 0.1 dynamic_slice.7
  79.3 0.1 dynamic_slice.6
  79.4 1.8 copy.46
  81.2 2.0 compare_and_fusion
  83.2 2.6 convolution_convert_fusion.2
  85.9 0.0 reduce-scatter.7.cloned.1.call-start
  85.9 49.3 %all-gather.8.cloned.1.call-done = bf16[6144,128]{1,0:T(8,128)(2,1)} async-done(((bf16[192,128]{1,0:T(8,128)(2,1)}), bf16[6144,128]{1,0:T(8,128)(2,1)}) %all-gather.8.cloned.1.call-update) | async-done | bytes 1572880 | tf_op jit(solution)/shard_map/all_gather | solution.py:55
  135.3 11.6 %fusion.2 = (f32[192,5]{0,1:T(8,128)S(1)}, f32[6144,192,5]{0,1,2:T(8,128)}) fusion(pred[192,6144]{1,0:T(8,128)(4,1)} %compare_and_fusion, bf16[192,5,128]{0,2,1:T(8,128)(2,1)} %bitcast.161, bf16[6144,128]{1,0:T(8,128)(2,1)} %all-gather.8.cloned.1.call-done), kind=kOutput, calls=%fused_computation.7 | convolution fusion | flops 1527643136 | bytes 26595072 | tf_op jit(solution)/shard_map/sgjd,ngd->sgjn/dot_general | solution.py:47
  146.9 11.4 %fusion.8 = f32[192,5]{0,1:T(8,128)S(1)} fusion(f32[6144,192,5]{0,1,2:T(8,128)} %get-tuple-element.28, f32[192,5]{0,1:T(8,128)S(1)} %broadcast_maximum_fusion, pred[192,6144]{1,0:T(8,128)(4,1)S(1)} %copy-done.3), kind=kLoop, calls=%fused_computation.13 | loop fusion | flops 23592000 | bytes 24780288 | tf_op jit(solution)/shard_map/reduce_sum | solution.py:69
  158.3 43.2 %all-gather.6.cloned.1.call-done = bf16[6144,128]{1,0:T(8,128)(2,1)} async-done(((bf16[192,128]{1,0:T(8,128)(2,1)}), bf16[6144,128]{1,0:T(8,128)(2,1)}) %all-gather.6.cloned.1.call-update) | async-done | bytes 1572880 | tf_op jit(solution)/shard_map/all_gather | solution.py:56
  201.5 13.0 %multiply_reduce_fusion = (f32[192,5]{0,1:T(8,128)S(1)}, bf16[192,1,5,128]{3,0,2,1:T(8,128)(2,1)S(1)}) fusion(f32[192,1,5,128]{3,0,2,1:T(8,128)} %copy.52, f32[192,5]{0,1:T(8,128)S(1)} %fusion.8, f32[6144,192,5]{0,1,2:T(8,128)} %get-tuple-element.28, f32[192,5]{0,1:T(8,128)S(1)} %broadcast_maximum_fusion, pred[192,6144]{1,0:T(8,128)(4,1)} %compare_and_fusion, ...), kind=kOutput, calls=%fused_computation.49 | convolution fusion | flops 1534155776 | bytes 27094272 | tf_op jit(solution)/shard_map/sgjn,ngd->sgjd/dot_general | solution.py:63
  214.5 19.3 %fusion.1 = bf16[192,1,5,6144]{3,0,2,1:T(8,128)(2,1)} fusion(f32[6144,192,5]{0,1,2:T(8,128)} %get-tuple-element.28, bf16[192,5,128]{0,2,1:T(8,128)(2,1)} %bitcast.159, f32[192,5]{0,1:T(8,128)S(1)} %get-tuple-element.29, f32[192,5]{0,1:T(8,128)S(1)} %log_add_fusion, pred[192,6144]{1,0:T(8,128)(4,1)} %compare_and_fusion, ...), kind=kOutput, calls=%fused_computation.2 | convolution fusion | flops 1551237120 | bytes 38395392 | tf_op jit(solution)/shard_map/sgjd,ngd->sgjn/dot_general | solution.py:82
  233.8 9.9 %fusion.31 = bf16[6144,128]{1,0:T(8,128)(2,1)} fusion(bf16[192,5,128]{0,2,1:T(8,128)(2,1)} %bitcast.162, bf16[192,1,5,6144]{3,0,2,1:T(8,128)(2,1)} %fusion.1), kind=kOutput, calls=%fused_computation.28 | convolution fusion | flops 1510735872 | bytes 13615104 | tf_op jit(solution)/shard_map/sgjn,sgjd->ngd/dot_general | solution.py:93
  243.7 0.0 reduce-scatter.9.cloned.1.call-start
  243.8 12.6 %fusion.28 = bf16[6144,128]{1,0:T(8,128)(2,1)} fusion(bf16[192,5,128]{0,2,1:T(8,128)(2,1)} %bitcast.160, f32[6144,192,5]{0,1,2:T(8,128)} %get-tuple-element.28, f32[192,5]{0,1:T(8,128)S(1)} %log_add_fusion, pred[192,6144]{1,0:T(8,128)(4,1)} %compare_and_fusion), kind=kOutput, calls=%fused_computation.27 | convolution fusion | flops 1534328832 | bytes 26595072 | tf_op jit(solution)/shard_map/sgjn,sgjd->ngd/dot_general | solution.py:87
  256.4 0.0 reduce-scatter.9.cloned.1.call-update
  256.4 0.0 reduce-scatter.13.cloned.1.call-start
  256.4 100.9 %reduce-scatter.7.cloned.1.call-done = bf16[192,128]{1,0:T(8,128)(2,1)} async-done(((bf16[6144,128]{1,0:T(8,128)(2,1)}), bf16[192,128]{1,0:T(8,128)(2,1)}) %reduce-scatter.7.cloned.1.call-update) | async-done | bytes 49168 | tf_op jit(solution)/shard_map/reduce_scatter | solution.py:100
  357.4 120.2 %reduce-scatter.9.cloned.1.call-done = bf16[192,128]{1,0:T(8,128)(2,1)} async-done(((bf16[6144,128]{1,0:T(8,128)(2,1)}), bf16[192,128]{1,0:T(8,128)(2,1)}) %reduce-scatter.9.cloned.1.call-update) | async-done | bytes 49168 | tf_op jit(solution)/shard_map/reduce_scatter | solution.py:103
  477.6 3.2 fusion.35
  480.8 4.4 copy.64
  485.2 0.0 reduce-scatter.13.cloned.1.call-update
  485.3 0.0 reduce-scatter.11.cloned.1.call-start
  485.3 0.7 fusion.88
  486.0 0.6 copy-done.2
  486.5 2.0 fusion.34
  488.6 0.2 copy.48
  488.8 0.9 copy.56
  489.6 0.4 copy-done.4
  490.0 6.1 fusion.51
  496.2 0.2 copy.53
  496.3 0.9 copy.57
  497.2 107.8 %reduce-scatter.13.cloned.1.call-done = bf16[160,256]{1,0:T(8,128)(2,1)} async-done(((bf16[5120,256]{1,0:T(8,128)(2,1)}), bf16[160,256]{1,0:T(8,128)(2,1)}) %reduce-scatter.13.cloned.1.call-update) | async-done | bytes 81936
  605.0 1.0 copy.65
  606.1 0.7 copy.58
  606.8 0.7 copy.59
  607.5 87.4 %reduce-scatter.11.cloned.1.call-done = bf16[24,5120]{1,0:T(8,128)(2,1)} async-done(((bf16[192,5120]{1,0:T(8,128)(2,1)}), bf16[24,5120]{1,0:T(8,128)(2,1)}) %reduce-scatter.11.cloned.1.call-update) | async-done | bytes 245776 | tf_op jit(solution)/shard_map/reduce_scatter | solution.py:109
  (26 shorter events, 0.1 us)
Async XLA Ops:
  7.2 63.6 %copy-start = (bf16[5120,128]{1,0:T(8,128)(2,1)S(1)}, bf16[5120,128]{1,0:T(8,128)(2,1)}, u32[]{:S(2)}) copy-start(bf16[5120,128]{1,0:T(8,128)(2,1)} %param.9) | copy-start | bytes 3932164
  7.2 68.6 %copy-start.5 = (bf16[192,640]{1,0:T(8,128)(2,1)S(1)}, bf16[192,640]{1,0:T(8,128)(2,1)}, u32[]{:S(2)}) copy-start(bf16[192,640]{1,0:T(8,128)(2,1)} %param.11) | copy-start | bytes 737284
  7.2 71.7 %copy-start.9 = (s32[64]{0:T(128)S(1)}, s32[64]{0:T(128)}, u32[]{:S(2)}) copy-start(s32[64]{0:T(128)} %param.12) | copy-start | bytes 772
  7.2 72.1 %copy-start.8 = (s32[6144]{0:T(1024)S(1)}, s32[6144]{0:T(1024)}, u32[]{:S(2)}) copy-start(s32[6144]{0:T(1024)} %param.13) | copy-start | bytes 73732
  7.2 63.6 %all-gather.4.cloned.1.call-start = ((), (), s32[]{:S(2)}) async-start(), calls=%async_computation.4 | async-start | bytes 2211840 | tf_op jit(solution)/shard_map/all_gather | solution.py:14
  7.9 127.3 %all-gather.8.cloned.1.call-start = ((), (), s32[]{:S(2)}) async-start(), calls=%async_computation.6 | async-start | bytes 1622016 | tf_op jit(solution)/shard_map/all_gather | solution.py:55
  70.8 12.4 %copy-start.1 = (bf16[192,5120]{1,0:T(8,128)(2,1)S(1)}, bf16[192,5120]{1,0:T(8,128)(2,1)}, u32[]{:S(2)}) copy-start(bf16[192,5120]{1,0:T(8,128)(2,1)} %all-gather.4.cloned.1.call-done) | copy-start | bytes 5898244
  73.8 127.7 %all-gather.6.cloned.1.call-start = ((), (), s32[]{:S(2)}) async-start(), calls=%async_computation.5 | async-start | bytes 1622016 | tf_op jit(solution)/shard_map/all_gather | solution.py:56
  85.9 271.5 %reduce-scatter.7.cloned.1.call-start = ((), (), s32[]{:S(2)}) async-start(), calls=%async_computation.7 | async-start | bytes 1622016 | tf_op jit(solution)/shard_map/reduce_scatter | solution.py:100
  135.3 11.6 %copy-start.3 = (pred[192,6144]{1,0:T(8,128)(4,1)S(1)}, pred[192,6144]{1,0:T(8,128)(4,1)}, u32[]{:S(2)}) copy-start(pred[192,6144]{1,0:T(8,128)(4,1)} %compare_and_fusion) | copy-start | bytes 3538948
  243.7 233.9 %reduce-scatter.9.cloned.1.call-start = ((), (), s32[]{:S(2)}) async-start(), calls=%async_computation.8 | async-start | bytes 1622016 | tf_op jit(solution)/shard_map/reduce_scatter | solution.py:103
  256.4 348.7 %reduce-scatter.13.cloned.1.call-start = ((), (), s32[]{:S(2)}) async-start(), calls=%async_computation.10 | async-start | bytes 2703360
  480.8 4.5 copy-start.6
  485.2 1.3 copy-start.2
  485.2 1.3 copy-start.7
  485.3 209.7 %reduce-scatter.11.cloned.1.call-start = ((), (), s32[]{:S(2)}) async-start(), calls=%async_computation.9 | async-start | bytes 2211840 | tf_op jit(solution)/shard_map/reduce_scatter | solution.py:109
  488.5 1.5 copy-start.4
Sparse Core Ops, SparseCore 0:
  10.6 60.1 all-gather.3
  73.9 61.2 all-gather.7
  137.7 63.7 all-gather.5
  243.9 113.4 reduce-scatter.6
  359.7 117.8 reduce-scatter.8
  485.4 119.6 reduce-scatter.12
  609.6 85.2 reduce-scatter.10
where the time goes:
time: 702 us
  waiting for transfers between devices  573 us (82%)
  matrix products  83.9 us (12%)
  local copies, waits for them, and re-layouts  16.9 us (2%)
  between operations  14.3 us (2%)
  other arithmetic  13.8 us (2%)
    reduce_scatter x1, waiting for transfers between devices, on_device(): lax.psum_scatter(grad_v_buf.astype(jnp.bfloat16), 'context', scatter_dime...  120 us
    unnamed x8, waiting for transfers between devices  109 us
    reduce_scatter x1, waiting for transfers between devices, on_device(): lax.psum_scatter(grad_k_buf.astype(jnp.bfloat16), 'context', scatter_dime...  101 us
    reduce_scatter x1, waiting for transfers between devices, on_device(): lax.psum_scatter((jnp.dot(grad_k_low, key_weight.T, preferred_element_typ...  87.4 us
    all_gather x1, waiting for transfers between devices, on_device(): local_rows = lax.all_gather(activations, 'tensor', axis=0, tiled=True)  62.8 us
    all_gather x1, waiting for transfers between devices, on_device(): key_piece = lax.all_gather(key_local, 'context', axis=0, tiled=True)  49.3 us
    all_gather x1, waiting for transfers between devices, on_device(): value_piece = lax.all_gather(value_local, 'context', axis=0, tiled=True)  43.2 us
    dot_general x1, matrix products, on_device(): jnp.einsum('sgjd,ngd->sgjn', grad_heads, value_heads_split, preferred_ele...  19.3 us
  transfers between devices with their start and end apart: 7, of which 7 were waited for; matrix products, arithmetic and copies ran while one was open for 9% of the time, Pallas kernels for 0%

commit v1 on v0

--- a/solution.py
+++ b/solution.py
@@ -52,8 +52,13 @@
 
     stats_shape = (shard_len, kv_heads, heads_per_group)
     run_max = jnp.full(stats_shape, -1e30, jnp.float32)
-    key_piece = lax.all_gather(key_local, "context", axis=0, tiled=True)
-    value_piece = lax.all_gather(value_local, "context", axis=0, tiled=True)
+    key_piece, value_piece = jnp.split(
+        lax.all_gather(
+            jnp.concatenate([key_local, value_local], axis=1), "context", axis=0, tiled=True
+        ),
+        [key_local.shape[1]],
+        axis=1,
+    )
     piece_len = key_piece.shape[0]
     pair_mask = visible()
     scores = scores_of(key_piece.reshape(piece_len, kv_heads, head_dim))

time: 702 us -> 753 us (1.073)
  waiting for transfers between devices: 573 us -> 618 us
  matrix products: 83.9 us -> 94.1 us
    all_gather x0 -> x1, waiting for transfers between devices: none -> 55.4 us  [on_device(): lax.all_gather(jnp.concatenate([key_local, value_local], axis=1), 'contex...]
    all_gather x1, waiting for transfers between devices: 43.2 us -> 28.9 us  [on_device(): value_piece = lax.all_gather(value_local, 'context', axis=0, tiled=True)]
    dot_general x1 -> x2, matrix products: 11.6 us -> 23.6 us  [scores_of(): jnp.einsum('sgjd,ngd->sgjn', query_heads, key_heads_split, preferred_elem...]
    unnamed x8 -> x9, waiting for transfers between devices: 109 us -> 108 us
  transfers between devices with their start and end apart: 7 -> 8, of which waited for: 7 -> 8; matrix products, arithmetic and copies ran while one was open for 9% -> 11% of each run, Pallas kernels for 0% -> 0%
where the time goes in v1:
time: 753 us
  waiting for transfers between devices  618 us (82%)
  matrix products  94.1 us (12%)
  other arithmetic  14.8 us (2%)
  between operations  14.3 us (2%)
  local copies, waits for them, and re-layouts  11.3 us (2%)
    reduce_scatter x1, waiting for transfers between devices, on_device(): lax.psum_scatter(grad_v_buf.astype(jnp.bfloat16), 'context', scatter_dime...  120 us
    unnamed x9, waiting for transfers between devices  108 us
    reduce_scatter x1, waiting for transfers between devices, on_device(): lax.psum_scatter(grad_k_buf.astype(jnp.bfloat16), 'context', scatter_dime...  101 us
    reduce_scatter x1, waiting for transfers between devices, on_device(): lax.psum_scatter((jnp.dot(grad_k_low, key_weight.T, preferred_element_typ...  87.5 us
    all_gather x1, waiting for transfers between devices, on_device(): local_rows = lax.all_gather(activations, 'tensor', axis=0, tiled=True)  62.8 us
    all_gather x1, waiting for transfers between devices, on_device(): lax.all_gather(jnp.concatenate([key_local, value_local], axis=1), 'contex...  55.4 us
    all_gather x1, waiting for transfers between devices, on_device(): key_piece = lax.all_gather(key_local, 'context', axis=0, tiled=True)  53.9 us
    all_gather x1, waiting for transfers between devices, on_device(): value_piece = lax.all_gather(value_local, 'context', axis=0, tiled=True)  28.9 us
  transfers between devices with their start and end apart: 8, of which 8 were waited for; matrix products, arithmetic and copies ran while one was open for 11% of the time, Pallas kernels for 0%

profile of v1, /device:TPU:32, one launch (start us, length us, event | category | flops | bytes accessed | tf_op | source)
XLA Modules:
  0.0 752.8 jit_solution(8677446344581257144)
XLA Ops:
  7.2 0.7 all-gather.5.cloned.1.call-update
  7.9 0.0 all-gather.9.cloned.1.call-start
  8.0 62.8 %all-gather.5.cloned.1.call-done = bf16[192,5120]{1,0:T(8,128)(2,1)} async-done(((bf16[24,5120]{1,0:T(8,128)(2,1)}), bf16[192,5120]{1,0:T(8,128)(2,1)}) %all-gather.5.cloned.1.call-update) | async-done | bytes 1966096 | tf_op jit(solution)/shard_map/all_gather | solution.py:14
  70.8 2.8 convolution_convert_fusion.2
  73.6 0.0 all-gather.7.cloned.1.call-start
  73.7 2.6 convolution_convert_fusion.1
  76.4 1.5 pad_maximum_fusion
  77.8 0.0 all-gather.11.cloned.1.call-start
  77.9 0.2 copy.55
  78.1 0.9 copy.53
  79.0 0.2 copy.56
  79.3 0.3 select_reduce_fusion
  79.6 0.1 dynamic_slice.7
  79.7 0.1 dynamic_slice.6
  79.8 0.2 copy.49
  80.0 1.0 compare_and_fusion
  81.0 0.2 reduce-scatter.7.cloned.1.call-start
  81.2 53.9 %all-gather.9.cloned.1.call-done = bf16[6144,128]{1,0:T(8,128)(2,1)} async-done(((bf16[192,128]{1,0:T(8,128)(2,1)}), bf16[6144,128]{1,0:T(8,128)(2,1)}) %all-gather.9.cloned.1.call-update) | async-done | bytes 1572880 | tf_op jit(solution)/shard_map/all_gather | solution.py:78
  135.1 12.5 %fusion.38 = f32[6144,192,5]{0,1,2:T(8,128)} fusion(bf16[192,5,128]{0,2,1:T(8,128)(2,1)S(1)} %bitcast.176, bf16[6144,128]{1,0:T(8,128)(2,1)} %all-gather.9.cloned.1.call-done), kind=kOutput, calls=%fused_computation.39 | convolution fusion | flops 1509949440 | bytes 25411584 | tf_op jit(solution)/shard_map/sgjd,ngd->sgjn/dot_general | solution.py:47
  147.6 55.4 %all-gather.7.cloned.1.call-done = bf16[6144,256]{1,0:T(8,128)(2,1)} async-done(((bf16[192,256]{1,0:T(8,128)(2,1)}), bf16[6144,256]{1,0:T(8,128)(2,1)}) %all-gather.7.cloned.1.call-update) | async-done | bytes 3145744 | tf_op jit(solution)/shard_map/all_gather | solution.py:56
  203.0 11.1 %fusion.3 = (f32[192,5]{0,1:T(8,128)S(1)}, f32[6144,192,5]{0,1,2:T(8,128)}) fusion(pred[192,6144]{1,0:T(8,128)(4,1)S(1)} %compare_and_fusion, bf16[192,5,128]{0,2,1:T(8,128)(2,1)S(1)} %bitcast.177, bf16[6144,256]{1,0:T(8,128)(2,1)} %all-gather.7.cloned.1.call-done), kind=kOutput, calls=%fused_computation.9 | convolution fusion | flops 1527643136 | bytes 26595072 | tf_op jit(solution)/shard_map/sgjd,ngd->sgjn/dot_general | solution.py:47
  214.1 11.4 %fusion.6 = f32[192,5]{0,1:T(8,128)S(1)} fusion(f32[6144,192,5]{0,1,2:T(8,128)} %get-tuple-element.28, f32[192,5]{0,1:T(8,128)S(1)} %broadcast_maximum_fusion, pred[192,6144]{1,0:T(8,128)(4,1)S(1)} %compare_and_fusion), kind=kLoop, calls=%fused_computation.12 | loop fusion | flops 23592000 | bytes 24780288 | tf_op jit(solution)/shard_map/reduce_sum | solution.py:74
  225.6 0.6 copy-done.9
  226.2 0.6 log_add_fusion
  226.8 13.2 %multiply_reduce_fusion = (f32[192,5]{0,1:T(8,128)}, bf16[192,1,5,128]{3,0,2,1:T(8,128)(2,1)S(1)}) fusion(f32[192,1,5,128]{3,0,2,1:T(8,128)S(1)} %copy.56, f32[192,5]{0,1:T(8,128)} %copy-done.9, f32[6144,192,5]{0,1,2:T(8,128)} %get-tuple-element.28, f32[192,5]{0,1:T(8,128)} %copy-done.10, pred[192,6144]{1,0:T(8,128)(4,1)S(1)} %compare_and_fusion, ...), kind=kOutput, calls=%fused_computation.51 | convolution fusion | flops 1534155776 | bytes 27102976 | tf_op jit(solution)/shard_map/sgjn,ngd->sgjd/dot_general | solution.py:68
  239.9 28.9 %all-gather.11.cloned.1.call-done = bf16[6144,128]{1,0:T(8,128)(2,1)} async-done(((bf16[192,128]{1,0:T(8,128)(2,1)}), bf16[6144,128]{1,0:T(8,128)(2,1)}) %all-gather.11.cloned.1.call-update) | async-done | bytes 1572880 | tf_op jit(solution)/shard_map/all_gather | solution.py:79
  268.9 15.8 %fusion.1 = bf16[192,1,5,6144]{3,0,2,1:T(8,128)(2,1)} fusion(f32[6144,192,5]{0,1,2:T(8,128)} %fusion.38, bf16[192,5,128]{0,2,1:T(8,128)(2,1)} %bitcast.181, f32[192,5]{0,1:T(8,128)} %get-tuple-element.29, f32[192,5]{0,1:T(8,128)} %log_add_fusion, pred[192,6144]{1,0:T(8,128)(4,1)S(1)} %compare_and_fusion, bf16[6144,128]{1,0:T(8,128)(2,1)} %all-gather.11.cloned.1.call-done), kind=kOutput, calls=%fused_computation.2 | convolution fusion | flops 1551237120 | bytes 38395392 | tf_op jit(solution)/shard_map/sgjd,ngd->sgjn/dot_general | solution.py:87
  284.6 9.9 %fusion.30 = bf16[6144,128]{1,0:T(8,128)(2,1)} fusion(bf16[192,5,128]{0,2,1:T(8,128)(2,1)S(1)} %bitcast.178, bf16[192,1,5,6144]{3,0,2,1:T(8,128)(2,1)} %fusion.1), kind=kOutput, calls=%fused_computation.28 | convolution fusion | flops 1510735872 | bytes 13615104 | tf_op jit(solution)/shard_map/sgjn,sgjd->ngd/dot_general | solution.py:98
  294.5 0.0 reduce-scatter.9.cloned.1.call-start
  294.6 12.7 %fusion.27 = bf16[6144,128]{1,0:T(8,128)(2,1)} fusion(bf16[192,5,128]{0,2,1:T(8,128)(2,1)} %bitcast.182, f32[6144,192,5]{0,1,2:T(8,128)} %fusion.38, f32[192,5]{0,1:T(8,128)S(1)} %copy-done.12, pred[192,6144]{1,0:T(8,128)(4,1)} %copy-done.3), kind=kOutput, calls=%fused_computation.27 | convolution fusion | flops 1534328832 | bytes 26595072 | tf_op jit(solution)/shard_map/sgjn,sgjd->ngd/dot_general | solution.py:92
  307.4 0.0 reduce-scatter.13.cloned.1.call-start
  307.4 100.8 %reduce-scatter.7.cloned.1.call-done = bf16[192,128]{1,0:T(8,128)(2,1)} async-done(((bf16[6144,128]{1,0:T(8,128)(2,1)}), bf16[192,128]{1,0:T(8,128)(2,1)}) %reduce-scatter.7.cloned.1.call-update) | async-done | bytes 49168 | tf_op jit(solution)/shard_map/reduce_scatter | solution.py:105
  408.2 120.1 %reduce-scatter.9.cloned.1.call-done = bf16[192,128]{1,0:T(8,128)(2,1)} async-done(((bf16[6144,128]{1,0:T(8,128)(2,1)}), bf16[192,128]{1,0:T(8,128)(2,1)}) %reduce-scatter.9.cloned.1.call-update) | async-done | bytes 49168 | tf_op jit(solution)/shard_map/reduce_scatter | solution.py:108
  528.3 3.2 fusion.34
  531.5 4.4 copy.69
  535.9 0.0 reduce-scatter.11.cloned.1.call-start
  536.0 0.7 fusion.79
  536.7 3.4 fusion.33
  540.1 0.2 copy.51
  540.3 0.9 copy.60
  541.2 6.1 fusion.48
  547.3 0.2 copy.57
  547.5 0.9 copy.61
  548.3 107.6 %reduce-scatter.13.cloned.1.call-done = bf16[160,256]{1,0:T(8,128)(2,1)} async-done(((bf16[5120,256]{1,0:T(8,128)(2,1)}), bf16[160,256]{1,0:T(8,128)(2,1)}) %reduce-scatter.13.cloned.1.call-update) | async-done | bytes 81936
  656.0 1.0 copy.70
  657.0 0.7 copy.62
  657.7 0.7 copy.63
  658.4 87.5 %reduce-scatter.11.cloned.1.call-done = bf16[24,5120]{1,0:T(8,128)(2,1)} async-done(((bf16[192,5120]{1,0:T(8,128)(2,1)}), bf16[24,5120]{1,0:T(8,128)(2,1)}) %reduce-scatter.11.cloned.1.call-update) | async-done | bytes 245776 | tf_op jit(solution)/shard_map/reduce_scatter | solution.py:114
  (39 shorter events, 0.3 us)
Async XLA Ops:
  7.2 63.6 %copy-start = (bf16[5120,128]{1,0:T(8,128)(2,1)S(1)}, bf16[5120,128]{1,0:T(8,128)(2,1)}, u32[]{:S(2)}) copy-start(bf16[5120,128]{1,0:T(8,128)(2,1)} %param.9) | copy-start | bytes 3932164
  7.2 70.7 %copy-start.4 = (bf16[192,640]{1,0:T(8,128)(2,1)S(1)}, bf16[192,640]{1,0:T(8,128)(2,1)}, u32[]{:S(2)}) copy-start(bf16[192,640]{1,0:T(8,128)(2,1)} %param.11) | copy-start | bytes 737284
  7.2 63.6 %all-gather.5.cloned.1.call-start = ((), (), s32[]{:S(2)}) async-start(), calls=%async_computation.4 | async-start | bytes 2211840 | tf_op jit(solution)/shard_map/all_gather | solution.py:14
  7.9 127.2 %all-gather.9.cloned.1.call-start = ((), (), s32[]{:S(2)}) async-start(), calls=%async_computation.6 | async-start | bytes 1622016 | tf_op jit(solution)/shard_map/all_gather | solution.py:78
  73.6 5.7 copy-start.13
  73.6 6.1 copy-start.11
  73.6 6.2 copy-start.6
  73.6 129.4 %all-gather.7.cloned.1.call-start = ((), (), s32[]{:S(2)}) async-start(), calls=%async_computation.5 | async-start | bytes 3244032 | tf_op jit(solution)/shard_map/all_gather | solution.py:56
  76.3 4.6 copy-start.5
  77.8 191.0 %all-gather.11.cloned.1.call-start = ((), (), s32[]{:S(2)}) async-start(), calls=%async_computation.7 | async-start | bytes 1622016 | tf_op jit(solution)/shard_map/all_gather | solution.py:79
  81.0 187.9 %copy-start.3 = (pred[192,6144]{1,0:T(8,128)(4,1)}, pred[192,6144]{1,0:T(8,128)(4,1)S(1)}, u32[]{:S(2)}) copy-start(pred[192,6144]{1,0:T(8,128)(4,1)S(1)} %compare_and_fusion) | copy-start | bytes 3538948
  81.0 327.2 %reduce-scatter.7.cloned.1.call-start = ((), (), s32[]{:S(2)}) async-start(), calls=%async_computation.8 | async-start | bytes 1622016 | tf_op jit(solution)/shard_map/reduce_scatter | solution.py:105
  214.1 11.4 %copy-start.10 = (f32[192,5]{0,1:T(8,128)}, f32[192,5]{0,1:T(8,128)S(1)}, u32[]{:S(2)}) copy-start(f32[192,5]{0,1:T(8,128)S(1)} %broadcast_maximum_fusion) | copy-start | bytes 11524
  225.6 0.6 copy-start.9
  284.6 10.0 %copy-start.12 = (f32[192,5]{0,1:T(8,128)S(1)}, f32[192,5]{0,1:T(8,128)}, u32[]{:S(2)}) copy-start(f32[192,5]{0,1:T(8,128)} %log_add_fusion) | copy-start | bytes 11524
  294.5 233.7 %copy-start.1 = (bf16[192,5120]{1,0:T(8,128)(2,1)S(1)}, bf16[192,5120]{1,0:T(8,128)(2,1)}, u32[]{:S(2)}) copy-start(bf16[192,5120]{1,0:T(8,128)(2,1)} %all-gather.5.cloned.1.call-done) | copy-start | bytes 5898244
  294.5 233.7 %reduce-scatter.9.cloned.1.call-start = ((), (), s32[]{:S(2)}) async-start(), calls=%async_computation.9 | async-start | bytes 1622016 | tf_op jit(solution)/shard_map/reduce_scatter | solution.py:108
  307.4 348.6 %reduce-scatter.13.cloned.1.call-start = ((), (), s32[]{:S(2)}) async-start(), calls=%async_computation.11 | async-start | bytes 2703360
  531.5 4.5 copy-start.7
  535.9 0.8 copy-start.8
  535.9 210.1 %reduce-scatter.11.cloned.1.call-start = ((), (), s32[]{:S(2)}) async-start(), calls=%async_computation.10 | async-start | bytes 2211840 | tf_op jit(solution)/shard_map/reduce_scatter | solution.py:114
  536.7 4.5 copy-start.2
Sparse Core Ops, SparseCore 0:
  10.6 60.1 all-gather.4
  73.8 61.2 all-gather.8
  137.6 65.4 all-gather.6
  205.3 63.5 all-gather.10
  294.7 113.4 reduce-scatter.6
  410.5 117.6 reduce-scatter.8
  536.0 119.8 reduce-scatter.12
  660.6 85.3 reduce-scatter.10
